TPU v7x, 256 devices: a whole 4x4x8 slice. The times are simulated.
256 devices in a mesh: expert: 64 (over y, z, core), dp: 4 (over x).
Axes of the slice: x: 4, y: 4, z: 8, core: 2. Of those that a mesh axis runs over, the one named last changes fastest.
Arguments:
- tokens: bfloat16 [32768, 1440], P(('expert', 'dp')), may hold values from -6 to 6
- routes: int32 [32768, 4], P(('expert', 'dp')), may hold values from 0 to 63, as said below
- gate_fixed: int32 [32768, 4], P(('expert', 'dp')), may hold values from 4096 to 65535
- counts: int32 [256], P(('expert', 'dp')), may hold values from 32 to 128, as said below
- replica_plan: int32 [8], replicated, may hold values from 0 to 63, as said below
- weight_in: bfloat16 [64, 1440, 1440], P('expert', None, 'dp'), may hold values from -0.15625 to 0.15625
- weight_out: bfloat16 [64, 1440, 1440], P('expert', 'dp'), may hold values from -0.15625 to 0.15625
- cotangent: bfloat16 [32768, 1440], P(('expert', 'dp')), may hold values from -0.59765625 to 0.59765625
Outputs:
- layer_output: bfloat16 [32768, 1440], P(('expert', 'dp'))
- input_grads: bfloat16 [32768, 1440], P(('expert', 'dp'))
- weight_in_grad: bfloat16 [64, 1440, 1440], P('expert', None, 'dp')
- weight_out_grad: bfloat16 [64, 1440, 1440], P('expert', 'dp')
Inputs may be any that keep to these rules, and one draw needn't show every extreme that they name: `routes`: each row names 4 different experts. `replica_plan`: 8 different experts, among them 0, 31, 32 and 63, in any order. `counts`: some device has 128 live tokens in every draw.
All inputs are finite; a program needn't handle non-finite values.
Results may differ from a plain program's by a relative error of at most 0.0064.
Values may be sent and summed in bfloat16 or wider, within the bound.
No kernel may reach another device: no remote copies, remote signals or barrier semaphores. Data moves between devices by JAX's collectives and lax.ppermute only.
A program may use at most 128 MiB of HBM per device.

v0:
```python
import jax
import jax.numpy as jnp
from jax import lax
from jax.sharding import PartitionSpec as P


def shifted(value, axis, steps):
    count = lax.axis_size(axis)
    pairs = [(source, (source + steps) % count) for source in range(count)]
    return lax.ppermute(value, axis, pairs)


def activate(values):
    return values * jax.nn.sigmoid(1.702 * values)


def derivative(values):
    sigmoid_value = jax.nn.sigmoid(1.702 * values)
    return sigmoid_value + 1.702 * values * sigmoid_value * (1.0 - sigmoid_value)


def slot_tables(routes, live_count, frequent_indicator, experts, capacity, spare_slots):
    token_count, top_count = routes.shape
    slot_width = capacity + spare_slots
    active = (jnp.arange(token_count, dtype=jnp.int32) < live_count).astype(jnp.int32)
    flattened = routes.reshape(-1)
    active_flat = jnp.repeat(active, top_count, total_repeat_length=token_count * top_count)
    same_expert = (flattened[:, None] == jnp.arange(experts, dtype=jnp.int32)[None, :]).astype(
        jnp.int32
    )
    matches = same_expert * active_flat[:, None]
    before = jnp.cumsum(matches, axis=0) - matches
    position = jnp.sum(before * matches, axis=1)
    hot_route = jnp.sum(same_expert * frequent_indicator[None, :], axis=1)
    keep_route = (active_flat > 0) & (position < capacity + spare_slots * hot_route)
    target_block = jnp.where(position < capacity, flattened, (flattened + experts // 2) % experts)
    slot_index = jnp.where(keep_route, target_block * slot_width + position, experts * slot_width)
    source = jnp.full((experts * slot_width + 1,), -1, jnp.int32)
    source = source.at[slot_index].set(jnp.arange(token_count * top_count, dtype=jnp.int32))
    return (slot_index, source[: experts * slot_width])


def gather_back(returned, slot_index, features):
    flattened = returned.reshape(-1, features)
    padded = jnp.concatenate([flattened, jnp.zeros((1, features), flattened.dtype)], axis=0)
    return padded[slot_index].astype(jnp.float32)


def slot_products(stacked, own_weight, copy_weight, dims, capacity, amount):
    width = stacked.shape[2]
    own_part = stacked[:, :capacity].reshape(-1, width)
    copy_part = stacked[:, capacity:].reshape(-1, width)
    own_term = lax.dot_general(own_part, own_weight, dims, preferred_element_type=jnp.float32)
    copy_term = lax.dot_general(copy_part, copy_weight, dims, preferred_element_type=jnp.float32)
    return jnp.concatenate(
        [
            own_term.reshape(amount, capacity, -1),
            copy_term.reshape(amount, stacked.shape[1] - capacity, -1),
        ],
        axis=1,
    )


def on_device(tokens, routes, gate_fixed, counts, replica_plan, weight_in, weight_out, cotangent):
    token_count, features = tokens.shape
    top_count = routes.shape[1]
    groups = lax.axis_size("expert")
    experts = groups * weight_in.shape[0]
    capacity = 3 * token_count * top_count // (8 * experts)
    spare_slots = capacity // 2
    slot_width = capacity + spare_slots
    contract_first = (((0,), (0,)), ((), ()))
    contract_last = (((1,), (1,)), ((), ()))
    contract_plain = (((1,), (0,)), ((), ()))
    frequent_indicator = jnp.sum(
        (replica_plan[:, None] == jnp.arange(experts, dtype=jnp.int32)[None, :]).astype(jnp.int32),
        axis=0,
    )
    slot_index, source = slot_tables(
        routes, counts[0], frequent_indicator, experts, capacity, spare_slots
    )
    filled = (source >= 0)[:, None]
    route_ids = jnp.maximum(source, 0)
    token_ids = route_ids // top_count
    scales = gate_fixed.reshape(-1).astype(jnp.float32) / 65536.0
    sent_rows = jnp.where(filled, tokens[token_ids], jnp.zeros((), jnp.bfloat16)).reshape(
        experts, slot_width, features
    )
    grad_rows = jnp.where(
        filled, scales[route_ids][:, None] * cotangent[token_ids].astype(jnp.float32), 0.0
    )
    grad_rows = grad_rows.astype(jnp.bfloat16).reshape(experts, slot_width, features)
    slab_in, slab_out = shifted((weight_in, weight_out), "expert", groups // 2)
    w_first = weight_in[0]
    w_second = weight_out[0]
    copy_first = slab_in[0]
    copy_second = slab_out[0]
    inbound = lax.all_to_all(sent_rows, "expert", split_axis=0, concat_axis=0, tiled=True)
    all_in = lax.all_gather(inbound, "dp", axis=0, tiled=True)
    blocks = all_in.shape[0]
    own_rows = all_in[:, :capacity].reshape(-1, features)
    copy_rows = all_in[:, capacity:].reshape(-1, features)
    own_pre = jnp.dot(own_rows, w_first, preferred_element_type=jnp.float32)
    copy_pre = jnp.dot(copy_rows, copy_first, preferred_element_type=jnp.float32)
    own_act = activate(own_pre).astype(jnp.bfloat16)
    copy_act = activate(copy_pre).astype(jnp.bfloat16)
    hidden_share = own_act.shape[1]
    act_all = jnp.concatenate(
        [
            own_act.reshape(blocks, capacity, hidden_share),
            copy_act.reshape(blocks, spare_slots, hidden_share),
        ],
        axis=1,
    )
    outputs = lax.psum_scatter(
        slot_products(
            act_all, w_second, copy_second, contract_plain, capacity, groups * lax.axis_size("dp")
        ),
        "dp",
        scatter_dimension=0,
        tiled=True,
    ).astype(jnp.bfloat16)
    returned = lax.all_to_all(outputs, "expert", split_axis=0, concat_axis=0, tiled=True)
    inbound_grad = lax.all_to_all(grad_rows, "expert", split_axis=0, concat_axis=0, tiled=True)
    all_grad = lax.all_gather(inbound_grad, "dp", axis=0, tiled=True)
    own_grad = all_grad[:, :capacity].reshape(-1, features)
    copy_grad = all_grad[:, capacity:].reshape(-1, features)
    own_act_grad = lax.dot_general(
        own_grad, w_second, contract_last, preferred_element_type=jnp.float32
    )
    copy_act_grad = lax.dot_general(
        copy_grad, copy_second, contract_last, preferred_element_type=jnp.float32
    )
    own_pre_grad = (own_act_grad * derivative(own_pre)).astype(jnp.bfloat16)
    copy_pre_grad = (copy_act_grad * derivative(copy_pre)).astype(jnp.bfloat16)
    pre_all = jnp.concatenate(
        [
            own_pre_grad.reshape(blocks, capacity, hidden_share),
            copy_pre_grad.reshape(blocks, spare_slots, hidden_share),
        ],
        axis=1,
    )
    input_rows = lax.psum_scatter(
        slot_products(
            pre_all, w_first, copy_first, contract_last, capacity, groups * lax.axis_size("dp")
        ),
        "dp",
        scatter_dimension=0,
        tiled=True,
    ).astype(jnp.bfloat16)
    copy_term_second = lax.dot_general(
        copy_act, copy_grad, contract_first, preferred_element_type=jnp.float32
    )
    copy_term_first = lax.dot_general(
        copy_rows, copy_pre_grad, contract_first, preferred_element_type=jnp.float32
    )
    home_second, home_first = (
        shifted(copy_term_second.astype(jnp.bfloat16), "expert", groups // 2).astype(
            copy_term_second.dtype
        ),
        shifted(copy_term_first.astype(jnp.bfloat16), "expert", groups // 2).astype(
            copy_term_first.dtype
        ),
    )
    grad_second = (
        lax.dot_general(own_act, own_grad, contract_first, preferred_element_type=jnp.float32)
        + home_second
    )
    grad_first = (
        lax.dot_general(own_rows, own_pre_grad, contract_first, preferred_element_type=jnp.float32)
        + home_first
    )
    weight_out_grad = grad_second.astype(jnp.bfloat16)[None]
    weight_in_grad = grad_first.astype(jnp.bfloat16)[None]
    returned_grad = lax.all_to_all(input_rows, "expert", split_axis=0, concat_axis=0, tiled=True)
    picked = gather_back(returned, slot_index, features) * scales[:, None]
    layer_output = jnp.sum(picked.reshape(token_count, top_count, features), axis=1).astype(
        jnp.bfloat16
    )
    picked_grad = gather_back(returned_grad, slot_index, features)
    input_grads = jnp.sum(picked_grad.reshape(token_count, top_count, features), axis=1).astype(
        jnp.bfloat16
    )
    return (layer_output, input_grads, weight_in_grad, weight_out_grad)


def solution(mesh):
    return jax.shard_map(
        on_device,
        mesh=mesh,
        in_specs=(
            P(("expert", "dp"), None),
            P(("expert", "dp"), None),
            P(("expert", "dp"), None),
            P(("expert", "dp")),
            P(),
            P("expert", None, "dp"),
            P("expert", "dp", None),
            P(("expert", "dp"), None),
        ),
        out_specs=(
            P(("expert", "dp"), None),
            P(("expert", "dp"), None),
            P("expert", None, "dp"),
            P("expert", "dp", None),
        ),
        check_vma=False,
    )
```

profile of v0, /device:TPU:1, one launch (start us, length us, event | category | flops | bytes accessed | tf_op | source)
XLA Modules:
  0.0 530.6 jit_solution(11869775184831770626)
XLA Ops:
  7.9 0.8 add_add_fusion.1
  8.7 3.3 gather_fusion
  12.8 1.2 reduce-window.14
  14.4 2.4 scatter_custom_fusion
  17.3 1.9 gather_fusion.3
  19.6 1.3 gather_fusion.4
  20.8 0.5 reshape.323
  21.3 0.4 select_convert_fusion
  21.8 36.2 %all_to_all.20 = bf16[64,4,1440]{2,1,0:T(4,128)(2,1)} all-to-all(bf16[64,4,1440]{2,1,0:T(4,128)(2,1)S(1)} %select_convert_fusion), channel_id=1, replica_groups=mesh['expert'=64,'dp'=4] {'expert'}, dimensions={0} | all-to-all | bytes 1474560 | tf_op jit(solution)/shard_map/all_to_all | solution.py:124
  58.2 1.3 gather_fusion.1
  59.7 0.4 broadcast_select_fusion
  60.1 29.1 %all_to_all.21 = bf16[64,4,1440]{2,1,0:T(4,128)(2,1)} all-to-all(bf16[64,4,1440]{2,1,0:T(4,128)(2,1)S(1)} %broadcast_select_fusion), channel_id=1, replica_groups=mesh['expert'=64,'dp'=4] {'expert'}, dimensions={0} | all-to-all | bytes 1474560 | tf_op jit(solution)/shard_map/all_to_all | solution.py:98
  89.2 2.9 collective-permute-start
  92.3 0.6 dynamic-slice.6
  93.5 3.5 all-gather.5.cloned.1.call-done
  97.1 3.6 slice.60
  100.7 3.3 copy.76
  104.0 37.2 %all-gather.3.cloned.1.call-done = bf16[256,4,1440]{2,1,0:T(4,128)(2,1)} async-done(((bf16[64,4,1440]{2,1,0:T(4,128)(2,1)}), bf16[256,4,1440]{2,1,0:T(4,128)(2,1)}) %all-gather.3.cloned.1.call-update) | async-done | bytes 2949136 | tf_op jit(solution)/shard_map/all_gather | solution.py:99
  141.2 4.9 slice.58
  146.1 4.6 copy.75
  150.7 4.1 reshape.318
  154.8 5.4 %reshape.314 = bf16[768,1440]{1,0:T(8,128)(2,1)S(1)} reshape(bf16[256,3,1440]{2,1,0:T(4,128)(2,1)} %bitcast.86) | data formatting | bytes 4423680 | tf_op jit(solution)/shard_map/reshape | solution.py:101
  160.2 3.3 multiply_convert_fusion
  163.6 2.6 fusion
  166.2 0.3 copy.67
  166.5 0.5 copy-done.9
  167.0 0.3 copy.59
  167.3 0.3 dot_general.41
  167.7 0.3 dot_general.46
  168.0 0.4 copy-done.1
  168.4 1.8 fusion.11
  170.3 2.7 fusion.6
  172.9 1.7 fusion.1
  174.7 1.8 convolution_bitcast_fusion
  176.5 2.9 pad_maximum_fusion.1
  179.4 7.9 %copy.70 = f32[256,4,1440]{2,1,0:T(4,128)} copy(f32[256,4,1440]{0,2,1:T(8,128)} %pad_maximum_fusion.1) | data formatting | bytes 11796480 | tf_op jit(solution)/shard_map/concatenate | solution.py:55
  187.3 2.6 fusion.4
  189.9 1.9 convolution_bitcast_fusion.1
  191.8 2.9 pad_maximum_fusion
  194.7 7.8 %copy.63 = f32[256,4,1440]{2,1,0:T(4,128)} copy(f32[256,4,1440]{0,2,1:T(8,128)} %pad_maximum_fusion) | data formatting | bytes 11796480 | tf_op jit(solution)/shard_map/concatenate | solution.py:55
  202.5 215.7 %all-reduce.6 = (bf16[256,4,1440]{2,1,0:T(4,128)(2,1)}, bf16[256,4,1440]{2,1,0:T(4,128)(2,1)}) all-reduce(f32[256,4,1440]{2,1,0:T(4,128)} %copy.63, f32[256,4,1440]{2,1,0:T(4,128)} %copy.70), channel_id=2, replica_groups=mesh['expert'=64,'dp'=4] {'dp'}, use_global_device_ids=true, to_apply=%region_6.7.clone | all-reduce | flops 2949120 | bytes 17694720
  418.2 2.3 dynamic-slice_convert_fusion.1
  420.4 12.4 %all-to-all-start.1 = ((bf16[64,4,1440]{2,1,0:T(4,128)(2,1)}), bf16[64,4,1440]{2,1,0:T(4,128)(2,1)S(1)}, u32[]{:S(2)}, u32[]{:S(2)}) async-start(bf16[64,4,1440]{2,1,0:T(4,128)(2,1)} %dynamic-slice_convert_fusion.1), calls=%async_computation.1 | async-start | bytes 1572864 | tf_op jit(solution)/shard_map/all_to_all | solution.py:123
  432.8 1.5 convolution_convert_fusion.1
  434.3 3.0 collective-permute-start.3
  437.3 2.3 dynamic-slice_convert_fusion
  439.6 16.1 %all-to-all-done.1 = bf16[64,4,1440]{2,1,0:T(4,128)(2,1)S(1)} async-done(((bf16[64,4,1440]{2,1,0:T(4,128)(2,1)}), bf16[64,4,1440]{2,1,0:T(4,128)(2,1)S(1)}, u32[]{:S(2)}, u32[]{:S(2)}) %all-to-all-start.1) | async-done | bytes 737312 | tf_op jit(solution)/shard_map/all_to_all | solution.py:123
  455.8 6.2 %all-to-all-start.3 = ((bf16[64,4,1440]{2,1,0:T(4,128)(2,1)}), bf16[64,4,1440]{2,1,0:T(4,128)(2,1)S(1)}, u32[]{:S(2)}, u32[]{:S(2)}) async-start(bf16[64,4,1440]{2,1,0:T(4,128)(2,1)} %dynamic-slice_convert_fusion), calls=%async_computation.3 | async-start | bytes 1572864 | tf_op jit(solution)/shard_map/all_to_all | solution.py:175
  462.0 0.6 convolution_convert_fusion
  462.6 3.1 collective-permute-start.2
  465.7 4.0 collective-permute-done.3
  469.7 4.0 fusion.3
  473.7 27.4 %collective-permute-done.2 = bf16[1440,360]{1,0:T(8,128)(2,1)S(1)} collective-permute-done((bf16[1440,360]{1,0:T(8,128)(2,1)S(1)}, bf16[1440,360]{1,0:T(8,128)(2,1)S(1)}, u32[]{:S(2)}, u32[]{:S(2)}) %collective-permute-start.2) | collective-permute-done | bytes 1036832 | tf_op jit(solution)/shard_map/ppermute | solution.py:10
  501.1 2.4 fusion.2
  503.5 0.4 reshape.317
  504.0 0.4 reshape.321
  504.4 3.2 gather_fusion.5
  507.6 2.9 gather.36
  510.5 2.2 reduce_sum.55
  512.7 0.9 copy.72
  513.6 3.0 gather_fusion.2
  516.6 2.9 reshape.322
  519.5 3.1 multiply_reduce_fusion
  522.6 0.9 copy.71
  (79 shorter events, 2.7 us)
Async XLA Ops:
  7.2 4.9 copy-start.15
  7.2 5.0 copy-start.16
  7.2 5.5 %copy-start.18 = (s32[8]{0:T(128)S(1)}, s32[8]{0:T(128)}, u32[]{:S(2)}) copy-start(s32[8]{0:T(128)} %param.14) | copy-start | bytes 100
  7.2 89.9 %all-gather.5.cloned.1.call-start = ((), (), s32[]{:S(2)}) async-start(), calls=%async_computation.5 | async-start | bytes 3932160 | tf_op jit(solution)/shard_map/all_gather | solution.py:125
  8.7 8.2 %copy-start.17 = (s32[128,4]{0,1:T(4,128)S(1)}, s32[128,4]{0,1:T(4,128)}, u32[]{:S(2)}) copy-start(s32[128,4]{0,1:T(4,128)} %param.12) | copy-start | bytes 6148
  12.1 7.3 %copy-start.13 = (bf16[128,1440]{0,1:T(8,128)(2,1)S(1)}, bf16[128,1440]{0,1:T(8,128)(2,1)}, u32[]{:S(2)}) copy-start(bf16[128,1440]{0,1:T(8,128)(2,1)} %param.17) | copy-start | bytes 1105924
  17.1 2.2 copy-start.8
  21.8 36.3 %copy-start.14 = (bf16[128,1440]{0,1:T(8,128)(2,1)S(1)}, bf16[128,1440]{0,1:T(8,128)(2,1)}, u32[]{:S(2)}) copy-start(bf16[128,1440]{0,1:T(8,128)(2,1)} %param.10) | copy-start | bytes 1105924
  58.0 83.2 %all-gather.3.cloned.1.call-start = ((), (), s32[]{:S(2)}) async-start(), calls=%async_computation.4 | async-start | bytes 3932160 | tf_op jit(solution)/shard_map/all_gather | solution.py:99
  60.1 32.2 %copy-start.19 = (u32[256]{0:T(256)S(1)}, u32[256]{0:T(256)}, u32[]{:S(2)}) copy-start(u32[256]{0:T(256)} %constant.170) | copy-start | bytes 3076
  89.2 78.8 %collective-permute-start = (bf16[1,1440,360]{2,1,0:T(8,128)(2,1)}, bf16[1,1440,360]{2,1,0:T(8,128)(2,1)}, u32[]{:S(2)}, u32[]{:S(2)}) collective-permute-start(bf16[1,1440,360]{2,1,0:T(8,128)(2,1)} %param.15), channel_id=1, source_target_pairs={{0,128},{4,132},{8,136},{12,140},{16,144},{20,148},{24,152},{28,15... | collective-permute-start | bytes 3110408 | tf_op jit(solution)/shard_map/ppermute | solution.py:10
  92.1 80.8 %collective-permute-start.1 = (bf16[1,360,1440]{2,1,0:T(8,128)(2,1)}, bf16[1,360,1440]{2,1,0:T(8,128)(2,1)}, u32[]{:S(2)}, u32[]{:S(2)}) collective-permute-start(bf16[1,360,1440]{2,1,0:T(8,128)(2,1)} %param.16), channel_id=1, source_target_pairs={{0,128},{4,132},{8,136},{12,140},{16,144},{20,148},{24,152},{28,15... | collective-permute-start | bytes 3110408 | tf_op jit(solution)/shard_map/ppermute | solution.py:10
  141.2 9.5 %copy-start = (bf16[256,4,1440]{2,1,0:T(4,128)(2,1)S(1)}, bf16[256,4,1440]{2,1,0:T(4,128)(2,1)}, u32[]{:S(2)}) copy-start(bf16[256,4,1440]{2,1,0:T(4,128)(2,1)} %all-gather.5.cloned.1.call-done) | copy-start | bytes 8847364
  160.2 3.3 copy-start.2
  160.2 3.4 copy-start.4
  163.5 3.0 copy-start.11
  166.2 0.8 copy-start.9
  167.3 1.1 copy-start.1
  170.2 2.7 copy-start.5
  174.6 4.8 copy-start.6
  420.4 35.3 %all-to-all-start.1 = ((bf16[64,4,1440]{2,1,0:T(4,128)(2,1)}), bf16[64,4,1440]{2,1,0:T(4,128)(2,1)S(1)}, u32[]{:S(2)}, u32[]{:S(2)}) async-start(bf16[64,4,1440]{2,1,0:T(4,128)(2,1)} %dynamic-slice_convert_fusion.1), calls=%async_computation.1 | async-start | bytes 1572864 | tf_op jit(solution)/shard_map/all_to_all | solution.py:123
  434.3 35.4 %collective-permute-start.3 = (bf16[360,1440]{1,0:T(8,128)(2,1)}, bf16[360,1440]{1,0:T(8,128)(2,1)}, u32[]{:S(2)}, u32[]{:S(2)}) collective-permute-start(bf16[360,1440]{1,0:T(8,128)(2,1)} %convolution_convert_fusion.1), channel_id=1, source_target_pairs={{0,128},{4,132},{8,136},{12,140},{16,144},{20,148},{24,152},{28,15... | collective-permute-start | bytes 3110408 | tf_op jit(solution)/shard_map/ppermute | solution.py:10
  437.3 24.7 %copy-start.7 = (bf16[256,360]{0,1:T(8,128)(2,1)S(1)}, bf16[256,360]{0,1:T(8,128)(2,1)}, u32[]{:S(2)}) copy-start(bf16[256,360]{0,1:T(8,128)(2,1)} %copy-done.6) | copy-start | bytes 552964
  439.6 30.0 %copy-start.12 = (bf16[768,360]{0,1:T(8,128)(2,1)S(1)}, bf16[768,360]{0,1:T(8,128)(2,1)}, u32[]{:S(2)}) copy-start(bf16[768,360]{0,1:T(8,128)(2,1)} %copy-done.11) | copy-start | bytes 1658884
  455.8 48.2 %all-to-all-start.3 = ((bf16[64,4,1440]{2,1,0:T(4,128)(2,1)}), bf16[64,4,1440]{2,1,0:T(4,128)(2,1)S(1)}, u32[]{:S(2)}, u32[]{:S(2)}) async-start(bf16[64,4,1440]{2,1,0:T(4,128)(2,1)} %dynamic-slice_convert_fusion), calls=%async_computation.3 | async-start | bytes 1572864 | tf_op jit(solution)/shard_map/all_to_all | solution.py:175
  462.6 38.5 %collective-permute-start.2 = (bf16[1440,360]{1,0:T(8,128)(2,1)S(1)}, bf16[1440,360]{1,0:T(8,128)(2,1)S(1)}, u32[]{:S(2)}, u32[]{:S(2)}) collective-permute-start(bf16[1440,360]{1,0:T(8,128)(2,1)S(1)} %convolution_convert_fusion), channel_id=1, source_target_pairs={{0,128},{4,132},{8,136},{12,140},{16,144},{20,148},{24,152},{28,15... | collective-permute-start | bytes 3110408 | tf_op jit(solution)/shard_map/ppermute | solution.py:10
  465.7 35.4 %copy-start.3 = (bf16[768,1440]{1,0:T(8,128)(2,1)S(1)}, bf16[768,1440]{1,0:T(8,128)(2,1)}, u32[]{:S(2)}) copy-start(bf16[768,1440]{1,0:T(8,128)(2,1)} %copy-done.2) | copy-start | bytes 6635524
  465.7 35.4 %copy-start.10 = (bf16[768,360]{0,1:T(8,128)(2,1)S(1)}, bf16[768,360]{0,1:T(8,128)(2,1)}, u32[]{:S(2)}) copy-start(bf16[768,360]{0,1:T(8,128)(2,1)} %copy-done.9) | copy-start | bytes 1658884
Sparse Core Ops, SparseCore 0:
  58.1 38.9 all-gather.4
  98.9 42.2 all-gather.2
where the time goes:
time: 540 us; the launch traced here: 531 us
  blocking collectives  281 us (52%)
  waiting for transfers between devices  88.3 us (16%)
  local copies, waits for them, and re-layouts  76.1 us (14%)
  starting transfers between devices  27.8 us (5%)
  matrix products  27 us (5%)
  between operations  16.2 us (3%)
  other arithmetic  14.4 us (3%)
    unnamed x1, blocking collectives  216 us
    all_gather x1, waiting for transfers between devices, on_device(): all_in = lax.all_gather(inbound, 'dp', axis=0, tiled=True)  37.2 us
    all_to_all x1, blocking collectives, on_device(): lax.all_to_all(grad_rows, 'expert', split_axis=0, concat_axis=0, tiled=True)  36.2 us
    ppermute x4, waiting for transfers between devices, shifted(): return lax.ppermute(value, axis, pairs)  31.4 us
    all_to_all x1, blocking collectives, on_device(): lax.all_to_all(sent_rows, 'expert', split_axis=0, concat_axis=0, tiled=True)  29.1 us
    all_to_all x1, waiting for transfers between devices, on_device(): lax.all_to_all(outputs, 'expert', split_axis=0, concat_axis=0, tiled=True)  16.1 us
    concatenate x2, local copies, waits for them, and re-layouts, slot_products(): jnp.concatenate([own_term.reshape(amount, capacity, -1), copy_term.reshap...  15.7 us
    all_to_all x1, starting transfers between devices, on_device(): lax.all_to_all(outputs, 'expert', split_axis=0, concat_axis=0, tiled=True)  12.4 us
  transfers between devices with their start and end apart: 8, of which 5 were waited for; matrix products, arithmetic and copies ran while one was open for 10% of the time, Pallas kernels for 0%

commit v1 on v0

--- a/solution.py
+++ b/solution.py
@@ -96,7 +96,9 @@
     copy_first = slab_in[0]
     copy_second = slab_out[0]
     inbound = lax.all_to_all(sent_rows, "expert", split_axis=0, concat_axis=0, tiled=True)
-    all_in = lax.all_gather(inbound, "dp", axis=0, tiled=True)
+    all_in = jnp.concatenate(
+        lax.all_to_all(jnp.stack([inbound] * lax.axis_size("dp")), "dp", 0, 0), axis=0
+    )
     blocks = all_in.shape[0]
     own_rows = all_in[:, :capacity].reshape(-1, features)
     copy_rows = all_in[:, capacity:].reshape(-1, features)

time: 540 us -> 567 us (1.050)
  blocking collectives: 281 us -> 216 us
  waiting for transfers between devices: 88.3 us -> 135 us
  starting transfers between devices: 27.8 us -> 52.2 us
  local copies, waits for them, and re-layouts: 76.1 us -> 90.3 us
    all_to_all x0 -> x3, waiting for transfers between devices: none -> 87.1 us  [the longest x1 44.8 us: on_device(): lax.all_to_all(jnp.stack([inbound] * lax.axis_size('dp')), 'dp', 0, 0)]
    all_to_all x2 -> x0, blocking collectives: 65.3 us -> none  [the longest x1 36.2 us: on_device(): lax.all_to_all(grad_rows, 'expert', split_axis=0, concat_axis=0, tiled=True)]
    all_gather x1 -> x0, waiting for transfers between devices: 37.2 us -> none  [on_device(): all_in = lax.all_gather(inbound, 'dp', axis=0, tiled=True)]
    all_to_all x0 -> x3, starting transfers between devices: none -> 24.1 us  [the longest x1 13.2 us: on_device(): lax.all_to_all(grad_rows, 'expert', split_axis=0, concat_axis=0, tiled=True)]
    unnamed x48 -> x39, local copies, waits for them, and re-layouts: 11.8 us -> 8.22 us
  transfers between devices with their start and end apart: 8 -> 10, of which waited for: 5 -> 6; matrix products, arithmetic and copies ran while one was open for 10% -> 10% of each run, Pallas kernels for 0% -> 0%
where the time goes in v1:
time: 567 us; the launch traced here: 558 us
  blocking collectives  216 us (38%)
  waiting for transfers between devices  135 us (24%)
  local copies, waits for them, and re-layouts  90.3 us (16%)
  starting transfers between devices  52.2 us (9%)
  matrix products  31 us (5%)
  other arithmetic  16.1 us (3%)
  between operations  16.1 us (3%)
    unnamed x1, blocking collectives  216 us
    all_to_all x1, waiting for transfers between devices, on_device(): lax.all_to_all(jnp.stack([inbound] * lax.axis_size('dp')), 'dp', 0, 0)  44.8 us
    ppermute x4, waiting for transfers between devices, shifted(): return lax.ppermute(value, axis, pairs)  32.8 us
    all_to_all x1, waiting for transfers between devices, on_device(): lax.all_to_all(sent_rows, 'expert', split_axis=0, concat_axis=0, tiled=True)  22.2 us
    all_to_all x1, waiting for transfers between devices, on_device(): lax.all_to_all(grad_rows, 'expert', split_axis=0, concat_axis=0, tiled=True)  20 us
    concatenate x2, local copies, waits for them, and re-layouts, slot_products(): jnp.concatenate([own_term.reshape(amount, capacity, -1), copy_term.reshap...  15.7 us
    all_to_all x1, waiting for transfers between devices, on_device(): lax.all_to_all(outputs, 'expert', split_axis=0, concat_axis=0, tiled=True)  15 us
    all_to_all x1, starting transfers between devices, on_device(): lax.all_to_all(grad_rows, 'expert', split_axis=0, concat_axis=0, tiled=True)  13.2 us
  transfers between devices with their start and end apart: 10, of which 6 were waited for; matrix products, arithmetic and copies ran while one was open for 10% of the time, Pallas kernels for 0%

profile of v1, /device:TPU:1, one launch (start us, length us, event | category | flops | bytes accessed | tf_op | source)
XLA Modules:
  0.0 557.6 jit_solution(2185654271285743948)
XLA Ops:
  7.9 0.8 add_add_fusion.1
  8.7 3.3 gather_fusion
  12.7 1.2 reduce-window.14
  14.4 2.4 scatter_custom_fusion
  17.3 1.9 gather_fusion.3
  19.5 1.3 gather_fusion.4
  21.3 1.3 select_convert_fusion
  22.6 13.2 %all-to-all-start.3 = ((bf16[64,4,1440]{2,1,0:T(4,128)(2,1)}), bf16[64,4,1440]{2,1,0:T(4,128)(2,1)S(1)}, u32[]{:S(2)}, u32[]{:S(2)}) async-start(bf16[64,4,1440]{2,1,0:T(4,128)(2,1)} %select_convert_fusion), calls=%async_computation.3 | async-start | bytes 1572864 | tf_op jit(solution)/shard_map/all_to_all | solution.py:126
  36.0 1.3 gather_fusion.1
  37.4 1.3 broadcast_select_fusion
  38.8 20.0 %all-to-all-done.3 = bf16[64,4,1440]{2,1,0:T(4,128)(2,1)S(1)} async-done(((bf16[64,4,1440]{2,1,0:T(4,128)(2,1)}), bf16[64,4,1440]{2,1,0:T(4,128)(2,1)S(1)}, u32[]{:S(2)}, u32[]{:S(2)}) %all-to-all-start.3) | async-done | bytes 737312 | tf_op jit(solution)/shard_map/all_to_all | solution.py:126
  58.8 6.2 %all-to-all-start = ((bf16[64,4,1440]{2,1,0:T(4,128)(2,1)}), bf16[64,4,1440]{2,1,0:T(4,128)(2,1)S(1)}, u32[]{:S(2)}, u32[]{:S(2)}) async-start(bf16[64,4,1440]{2,1,0:T(4,128)(2,1)} %broadcast_select_fusion), calls=%async_computation | async-start | bytes 1572864 | tf_op jit(solution)/shard_map/all_to_all | solution.py:98
  65.0 0.7 all-gather.2.cloned.1.call-update
  65.7 22.2 %all-to-all-done = bf16[64,4,1440]{2,1,0:T(4,128)(2,1)S(1)} async-done(((bf16[64,4,1440]{2,1,0:T(4,128)(2,1)}), bf16[64,4,1440]{2,1,0:T(4,128)(2,1)S(1)}, u32[]{:S(2)}, u32[]{:S(2)}) %all-to-all-start) | async-done | bytes 737312 | tf_op jit(solution)/shard_map/all_to_all | solution.py:98
  88.1 2.0 stack.2
  90.1 4.8 all-to-all-start.1
  94.9 2.9 collective-permute-start
  99.6 44.8 %all-to-all-done.1 = bf16[4,64,4,1440]{3,1,2,0:T(8,128)(2,1)} async-done(((bf16[4,64,4,1440]{3,1,2,0:T(8,128)(2,1)}), bf16[4,64,4,1440]{3,1,2,0:T(8,128)(2,1)}, u32[]{:S(2)}, u32[]{:S(2)}) %all-to-all-start.1) | async-done | bytes 2949152 | tf_op jit(solution)/shard_map/all_to_all | solution.py:100
  144.4 2.2 copy.83
  146.8 3.7 copy.84
  150.4 6.7 %reshape.320 = bf16[768,1440]{1,0:T(8,128)(2,1)} reshape(bf16[256,3,1440]{2,1,0:T(4,128)(2,1)} %copy.84) | data formatting | bytes 4423680 | tf_op jit(solution)/shard_map/reshape | solution.py:103
  157.1 4.3 multiply_convert_fusion
  161.5 2.1 copy.85
  163.6 2.0 dot_general.41
  165.6 1.8 fusion.11
  167.5 2.0 convolution_bitcast_fusion.1
  169.5 2.6 fusion.4
  172.1 2.9 pad_maximum_fusion
  175.0 7.9 %copy.89 = f32[256,4,1440]{2,1,0:T(4,128)} copy(f32[256,4,1440]{0,2,1:T(8,128)} %pad_maximum_fusion) | data formatting | bytes 11796480 | tf_op jit(solution)/shard_map/concatenate | solution.py:55
  182.9 4.7 slice.60
  187.6 4.6 copy.101
  192.1 6.7 %reshape.324 = bf16[768,1440]{1,0:T(8,128)(2,1)} reshape(bf16[256,3,1440]{2,1,0:T(4,128)(2,1)} %bitcast.89) | data formatting | bytes 4423680 | tf_op jit(solution)/shard_map/reshape | solution.py:128
  198.9 4.3 fusion
  203.2 2.1 copy.93
  205.3 2.0 dot_general.46
  207.3 2.9 fusion.6
  210.2 1.7 fusion.1
  211.9 0.7 copy-done.4
  212.6 1.8 convolution_bitcast_fusion
  214.4 2.9 pad_maximum_fusion.1
  217.2 7.9 %copy.96 = f32[256,4,1440]{2,1,0:T(4,128)} copy(f32[256,4,1440]{0,2,1:T(8,128)} %pad_maximum_fusion.1) | data formatting | bytes 11796480 | tf_op jit(solution)/shard_map/concatenate | solution.py:55
  225.1 216.5 %all-reduce.6 = (bf16[256,4,1440]{2,1,0:T(4,128)(2,1)}, bf16[256,4,1440]{2,1,0:T(4,128)(2,1)}) all-reduce(f32[256,4,1440]{2,1,0:T(4,128)} %copy.89, f32[256,4,1440]{2,1,0:T(4,128)} %copy.96), channel_id=2, replica_groups=mesh['expert'=64,'dp'=4] {'dp'}, use_global_device_ids=true, to_apply=%region_6.7.clone | all-reduce | flops 2949120 | bytes 17694720
  441.6 2.3 dynamic-slice_convert_fusion.1
  443.8 12.1 %all-to-all-start.2 = ((bf16[64,4,1440]{2,1,0:T(4,128)(2,1)}), bf16[64,4,1440]{2,1,0:T(4,128)(2,1)}, u32[]{:S(2)}, u32[]{:S(2)}) async-start(bf16[64,4,1440]{2,1,0:T(4,128)(2,1)} %dynamic-slice_convert_fusion.1), calls=%async_computation.2 | async-start | bytes 1572864 | tf_op jit(solution)/shard_map/all_to_all | solution.py:125
  455.9 2.6 convolution_convert_fusion.1
  458.5 3.0 collective-permute-start.3
  461.5 2.4 dynamic-slice_convert_fusion
  463.9 15.0 %all-to-all-done.2 = bf16[64,4,1440]{2,1,0:T(4,128)(2,1)} async-done(((bf16[64,4,1440]{2,1,0:T(4,128)(2,1)}), bf16[64,4,1440]{2,1,0:T(4,128)(2,1)}, u32[]{:S(2)}, u32[]{:S(2)}) %all-to-all-start.2) | async-done | bytes 737312 | tf_op jit(solution)/shard_map/all_to_all | solution.py:125
  478.8 6.4 %all-to-all-start.4 = ((bf16[64,4,1440]{2,1,0:T(4,128)(2,1)}), bf16[64,4,1440]{2,1,0:T(4,128)(2,1)}, u32[]{:S(2)}, u32[]{:S(2)}) async-start(bf16[64,4,1440]{2,1,0:T(4,128)(2,1)} %dynamic-slice_convert_fusion), calls=%async_computation.4 | async-start | bytes 1572864 | tf_op jit(solution)/shard_map/all_to_all | solution.py:177
  485.8 3.1 collective-permute-start.2
  488.9 5.9 %collective-permute-done.3 = bf16[360,1440]{1,0:T(8,128)(2,1)} collective-permute-done((bf16[360,1440]{1,0:T(8,128)(2,1)}, bf16[360,1440]{1,0:T(8,128)(2,1)}, u32[]{:S(2)}, u32[]{:S(2)}) %collective-permute-start.3) | collective-permute-done | bytes 1036832 | tf_op jit(solution)/shard_map/ppermute | solution.py:10
  494.8 4.0 fusion.3
  498.8 26.9 %collective-permute-done.2 = bf16[1440,360]{1,0:T(8,128)(2,1)S(1)} collective-permute-done((bf16[1440,360]{1,0:T(8,128)(2,1)S(1)}, bf16[1440,360]{1,0:T(8,128)(2,1)S(1)}, u32[]{:S(2)}, u32[]{:S(2)}) %collective-permute-start.2) | collective-permute-done | bytes 1036832 | tf_op jit(solution)/shard_map/ppermute | solution.py:10
  525.6 2.5 fusion.2
  528.1 1.8 reshape.323
  530.0 1.6 reshape.327
  531.6 3.0 gather_fusion.5
  534.6 2.9 gather.36
  537.5 2.2 reduce_sum.55
  539.7 0.9 copy.98
  540.6 3.0 gather_fusion.2
  543.5 2.9 reshape.328
  546.5 3.1 multiply_reduce_fusion
  549.6 0.9 copy.97
  (75 shorter events, 5.0 us)
Async XLA Ops:
  7.2 4.9 copy-start.11
  7.2 5.0 copy-start.12
  7.2 5.4 copy-start.14
  7.2 9.7 %copy-start.13 = (s32[128,4]{0,1:T(4,128)S(1)}, s32[128,4]{0,1:T(4,128)}, u32[]{:S(2)}) copy-start(s32[128,4]{0,1:T(4,128)} %param.12) | copy-start | bytes 6148
  12.0 7.3 %copy-start.9 = (bf16[128,1440]{0,1:T(8,128)(2,1)S(1)}, bf16[128,1440]{0,1:T(8,128)(2,1)}, u32[]{:S(2)}) copy-start(bf16[128,1440]{0,1:T(8,128)(2,1)} %param.17) | copy-start | bytes 1105924
  17.0 2.2 copy-start.6
  21.3 14.5 %copy-start.10 = (bf16[128,1440]{0,1:T(8,128)(2,1)S(1)}, bf16[128,1440]{0,1:T(8,128)(2,1)}, u32[]{:S(2)}) copy-start(bf16[128,1440]{0,1:T(8,128)(2,1)} %param.10) | copy-start | bytes 1105924
  22.6 36.1 %all-to-all-start.3 = ((bf16[64,4,1440]{2,1,0:T(4,128)(2,1)}), bf16[64,4,1440]{2,1,0:T(4,128)(2,1)S(1)}, u32[]{:S(2)}, u32[]{:S(2)}) async-start(bf16[64,4,1440]{2,1,0:T(4,128)(2,1)} %select_convert_fusion), calls=%async_computation.3 | async-start | bytes 1572864 | tf_op jit(solution)/shard_map/all_to_all | solution.py:126
  58.8 6.3 %copy-start = (bf16[64,4,1440]{2,1,0:T(4,128)(2,1)}, bf16[64,4,1440]{2,1,0:T(4,128)(2,1)S(1)}, u32[]{:S(2)}) copy-start(bf16[64,4,1440]{2,1,0:T(4,128)(2,1)S(1)} %all-to-all-done.3) | copy-start | bytes 2211844
  58.8 29.2 %all-to-all-start = ((bf16[64,4,1440]{2,1,0:T(4,128)(2,1)}), bf16[64,4,1440]{2,1,0:T(4,128)(2,1)S(1)}, u32[]{:S(2)}, u32[]{:S(2)}) async-start(bf16[64,4,1440]{2,1,0:T(4,128)(2,1)} %broadcast_select_fusion), calls=%async_computation | async-start | bytes 1572864 | tf_op jit(solution)/shard_map/all_to_all | solution.py:98
  65.0 117.9 %all-gather.2.cloned.1.call-start = ((), (), s32[]{:S(2)}) async-start(), calls=%async_computation.5 | async-start | bytes 3932160 | tf_op jit(solution)/shard_map/all_gather | solution.py:127
  90.1 8.3 %copy-start.15 = (u32[256]{0:T(256)S(1)}, u32[256]{0:T(256)}, u32[]{:S(2)}) copy-start(u32[256]{0:T(256)} %constant.170) | copy-start | bytes 3076
  90.1 54.3 %all-to-all-start.1 = ((bf16[4,64,4,1440]{3,1,2,0:T(8,128)(2,1)}), bf16[4,64,4,1440]{3,1,2,0:T(8,128)(2,1)}, u32[]{:S(2)}, u32[]{:S(2)}) async-start(bf16[4,64,4,1440]{3,1,2,0:T(8,128)(2,1)} %stack.2), calls=%async_computation.1 | async-start | bytes 6291456 | tf_op jit(solution)/shard_map/all_to_all | solution.py:100
  94.9 70.7 %collective-permute-start = (bf16[1,1440,360]{2,1,0:T(8,128)(2,1)}, bf16[1,1440,360]{2,1,0:T(8,128)(2,1)}, u32[]{:S(2)}, u32[]{:S(2)}) collective-permute-start(bf16[1,1440,360]{2,1,0:T(8,128)(2,1)} %param.15), channel_id=1, source_target_pairs={{0,128},{4,132},{8,136},{12,140},{16,144},{20,148},{24,152},{28,15... | collective-permute-start | bytes 3110408 | tf_op jit(solution)/shard_map/ppermute | solution.py:10
  97.8 69.7 %collective-permute-start.1 = (bf16[1,360,1440]{2,1,0:T(8,128)(2,1)}, bf16[1,360,1440]{2,1,0:T(8,128)(2,1)}, u32[]{:S(2)}, u32[]{:S(2)}) collective-permute-start(bf16[1,360,1440]{2,1,0:T(8,128)(2,1)} %param.16), channel_id=1, source_target_pairs={{0,128},{4,132},{8,136},{12,140},{16,144},{20,148},{24,152},{28,15... | collective-permute-start | bytes 3110408 | tf_op jit(solution)/shard_map/ppermute | solution.py:10
  167.5 2.0 copy-start.1
  207.3 2.9 copy-start.3
  211.9 0.7 copy-start.4
  443.8 35.0 %all-to-all-start.2 = ((bf16[64,4,1440]{2,1,0:T(4,128)(2,1)}), bf16[64,4,1440]{2,1,0:T(4,128)(2,1)}, u32[]{:S(2)}, u32[]{:S(2)}) async-start(bf16[64,4,1440]{2,1,0:T(4,128)(2,1)} %dynamic-slice_convert_fusion.1), calls=%async_computation.2 | async-start | bytes 1572864 | tf_op jit(solution)/shard_map/all_to_all | solution.py:125
  458.5 36.3 %collective-permute-start.3 = (bf16[360,1440]{1,0:T(8,128)(2,1)}, bf16[360,1440]{1,0:T(8,128)(2,1)}, u32[]{:S(2)}, u32[]{:S(2)}) collective-permute-start(bf16[360,1440]{1,0:T(8,128)(2,1)} %convolution_convert_fusion.1), channel_id=1, source_target_pairs={{0,128},{4,132},{8,136},{12,140},{16,144},{20,148},{24,152},{28,15... | collective-permute-start | bytes 3110408 | tf_op jit(solution)/shard_map/ppermute | solution.py:10
  461.5 23.7 %copy-start.5 = (bf16[256,360]{0,1:T(8,128)(2,1)S(1)}, bf16[256,360]{0,1:T(8,128)(2,1)}, u32[]{:S(2)}) copy-start(bf16[256,360]{0,1:T(8,128)(2,1)} %copy-done.4) | copy-start | bytes 552964
  478.8 51.1 %all-to-all-start.4 = ((bf16[64,4,1440]{2,1,0:T(4,128)(2,1)}), bf16[64,4,1440]{2,1,0:T(4,128)(2,1)}, u32[]{:S(2)}, u32[]{:S(2)}) async-start(bf16[64,4,1440]{2,1,0:T(4,128)(2,1)} %dynamic-slice_convert_fusion), calls=%async_computation.4 | async-start | bytes 1572864 | tf_op jit(solution)/shard_map/all_to_all | solution.py:177
  485.2 9.6 %copy-start.7 = (bf16[768,360]{0,1:T(8,128)(2,1)S(1)}, bf16[768,360]{0,1:T(8,128)(2,1)}, u32[]{:S(2)}) copy-start(bf16[768,360]{0,1:T(8,128)(2,1)} %get-tuple-element.32) | copy-start | bytes 1658884
  485.8 39.8 %collective-permute-start.2 = (bf16[1440,360]{1,0:T(8,128)(2,1)S(1)}, bf16[1440,360]{1,0:T(8,128)(2,1)S(1)}, u32[]{:S(2)}, u32[]{:S(2)}) collective-permute-start(bf16[1440,360]{1,0:T(8,128)(2,1)S(1)} %convolution_convert_fusion), channel_id=1, source_target_pairs={{0,128},{4,132},{8,136},{12,140},{16,144},{20,148},{24,152},{28,15... | collective-permute-start | bytes 3110408 | tf_op jit(solution)/shard_map/ppermute | solution.py:10
  488.9 36.7 %copy-start.2 = (bf16[768,1440]{1,0:T(8,128)(2,1)S(1)}, bf16[768,1440]{1,0:T(8,128)(2,1)}, u32[]{:S(2)}) copy-start(bf16[768,1440]{1,0:T(8,128)(2,1)} %reshape.320) | copy-start | bytes 6635524
  488.9 36.7 %copy-start.8 = (bf16[768,360]{0,1:T(8,128)(2,1)S(1)}, bf16[768,360]{0,1:T(8,128)(2,1)}, u32[]{:S(2)}) copy-start(bf16[768,360]{0,1:T(8,128)(2,1)} %fusion) | copy-start | bytes 1658884
Sparse Core Ops, SparseCore 0:
  67.6 54.1 all-gather.1
